TPU v7x, 32 devices: a whole 2x2x4 slice. The times are simulated.
32 devices in a mesh: wide: 8 (over z, x), narrow: 4 (over y, core).
Axes of the slice: x: 2, y: 2, z: 4, core: 2. Of those that a mesh axis runs over, the one named last changes fastest.
Arguments:
- pressure: float32 [1024, 128], P(('wide', 'narrow')), may hold values from -6 to 6
- right_side: float32 [1024, 128], P(('wide', 'narrow')), may hold values from -6 to 6
- concentration: float32 [1024, 128], P(('wide', 'narrow')), may hold values from 0 to 1
- pore_volume: float32 [1024, 128], P(('wide', 'narrow')), may hold values from 0.5 to 2
- well_rate: float32 [1024, 128], P(('wide', 'narrow')), may hold values from 0.02 to 0.5
- inject_conc: float32 [1024, 128], P(('wide', 'narrow')), may hold values from 0 to 1
- transmissibility: float32 [6, 131072], P(None, ('wide', 'narrow')), may hold values from 0.1 to 1
- face_neighbor: int32 [6, 1024], P(None, ('wide', 'narrow')), may hold values from 0 to 56, as said below
- sub_matrix: bfloat16 [2048, 4, 128, 128], P(('wide', 'narrow')), as said below
- sub_columns: int32 [2048, 4], P(('wide', 'narrow')), may hold values from 0 to 63, as said below
- send_blocks: int32 [32, 4, 8], P(('wide', 'narrow')), may hold values from 0 to 31, as said below
- send_counts: int32 [32, 4], P(('wide', 'narrow')), may hold values from 1 to 8, as said below
- basis_weights: bfloat16 [8192, 4096], P(('wide', 'narrow')), may hold values from -0.09375 to 0.09375
- coarse_index: int32 [8192], P(('wide', 'narrow')), may hold values from 0 to 4095, as said below
- coarse_inverse: float32 [4096, 512], P(('wide', 'narrow')), may hold values from -0.25 to 0.25
Outputs:
- pressure_new: float32 [1024, 128], P(('wide', 'narrow'))
- concentration_new: float32 [1024, 128], P(('wide', 'narrow'))
Inputs may be any that keep to these rules, and one draw needn't show every extreme that they name: `send_blocks`: local block indices below 32. `send_counts`: between 1 and 8; the first subdomain sends 8 blocks to every neighbour and the last sends one. `sub_columns`: slot 0 of each row block names the row block itself. `face_neighbor`: each owned block's faces name owned blocks or the first received block from some neighbour. `coarse_index`: a subdomain's functions may be owned by any index of wide, and may repeat. `sub_matrix`: the diagonal of each row block's first stored block lies between 0.9 and 2.1.
All inputs are finite; a program needn't handle non-finite values.
Results may differ from a plain program's by a relative error of at most 0.00225.
The roundings to bfloat16 on the way count: a program that leaves them out, or rounds other values in their place, can miss the bound.
Values may be sent and summed in bfloat16 or wider, within the bound.
A program may use at most 64 MiB of HBM per device.

v0:
```python
import jax
import jax.numpy as jnp
from jax import lax
from jax.sharding import PartitionSpec as P

SWEEPS = 4
shift_offsets = (2, 1, -1, -2)
courant = 0.9


def from_behind(value, axis, steps):
    count = lax.axis_size(axis)
    leading, last = (max(0, -steps), min(count, count - steps))
    return lax.ppermute(value, axis, [(source, source + steps) for source in range(leading, last)])


def block_product(matrix, columns, vector_b):
    picked = vector_b[columns]
    return jnp.einsum("rkij,rkj->ri", matrix, picked, preferred_element_type=jnp.float32)


def outgoing_one(owned_rows, send_blocks, send_counts):
    slot_count = send_blocks.shape[-1]
    active = jnp.arange(slot_count)[None, :] < send_counts[0][:, None]
    picked = owned_rows[send_blocks[0]]
    return jnp.where(active[:, :, None], picked, jnp.zeros_like(picked))


def with_rims(owned_list, send_blocks, send_counts, mover):
    packed = [outgoing_one(owned_rows, send_blocks, send_counts) for owned_rows in owned_list]
    arrived = [[owned_rows] for owned_rows in owned_list]
    for position, offset in enumerate(shift_offsets):
        moved_rows = mover([sent_rows[position] for sent_rows in packed], offset)
        for target, portion in zip(arrived, moved_rows):
            target.append(portion)
    return [jnp.concatenate(target, axis=0) for target in arrived]


def local(
    pressure,
    right_side,
    concentration,
    pore_volume,
    well_rate,
    inject_conc,
    transmissibility,
    face_neighbor,
    sub_matrix,
    sub_columns,
    send_blocks,
    send_counts,
    basis_weights,
    coarse_index,
    coarse_inverse,
):
    owned_count = pressure.shape[0]
    pressure_b = pressure.astype(jnp.bfloat16)
    ext_pressure = with_rims(
        [pressure_b],
        send_blocks,
        send_counts,
        lambda members, offset: (from_behind(members[0], "wide", offset),),
    )[0]
    residual = right_side - block_product(
        sub_matrix[:owned_count], sub_columns[:owned_count], ext_pressure
    )
    residual_b = residual.astype(jnp.bfloat16)
    local_coarse = jnp.dot(
        basis_weights, residual_b.reshape(-1), preferred_element_type=jnp.float32
    )
    coarse_width = coarse_inverse.shape[1]
    wide_count = lax.axis_size("wide")
    coarse_total = coarse_width * wide_count
    ext_residual = with_rims(
        [residual_b],
        send_blocks,
        send_counts,
        lambda members, offset: (from_behind(members[0], "wide", offset),),
    )[0]
    diagonal = jnp.diagonal(sub_matrix[:, 0], axis1=1, axis2=2).astype(jnp.float32)
    target_rows = ext_residual.astype(jnp.float32)
    update = jnp.zeros(target_rows.shape, jnp.float32)
    for turn_index in range(SWEEPS):
        update = (
            update
            + (target_rows - block_product(sub_matrix, sub_columns, update.astype(jnp.bfloat16)))
            / diagonal
        )
    partial_value = jnp.zeros((coarse_total,), jnp.float32).at[coarse_index].add(local_coarse)
    summed = lax.psum(partial_value, ("wide", "narrow"))
    owner_block = lax.dynamic_slice_in_dim(
        summed, lax.axis_index("wide") * coarse_width, coarse_width
    )
    block_inverse = lax.all_gather(coarse_inverse, "narrow", axis=0, tiled=True)
    owner_values = jnp.dot(block_inverse, owner_block, precision=lax.Precision.HIGHEST)
    coarse_values = lax.all_gather(owner_values, "wide", axis=0, tiled=True)
    picked_coarse = coarse_values.astype(jnp.bfloat16)[coarse_index]
    correction = jnp.dot(picked_coarse, basis_weights, preferred_element_type=jnp.float32)
    pressure_next = pressure + update[:owned_count] + correction.reshape(owned_count, -1)
    ext_next, ext_conc = with_rims(
        [pressure_next, concentration],
        send_blocks,
        send_counts,
        lambda members, offset: from_behind((members[0], members[1]), "wide", offset),
    )
    face_count = face_neighbor.shape[0]
    near_pressure = ext_next[face_neighbor].reshape(face_count, -1)
    near_conc = ext_conc[face_neighbor].reshape(face_count, -1)
    own_pressure = pressure_next.reshape(1, -1)
    conc_flat = concentration.reshape(-1)
    face_flux = transmissibility * (own_pressure - near_pressure)
    outward = jnp.maximum(face_flux, 0.0)
    inward = jnp.minimum(face_flux, 0.0)
    advection = jnp.sum(outward * conc_flat[None, :] + inward * near_conc, axis=0)
    outflow = jnp.sum(outward, axis=0)
    volume_flat = pore_volume.reshape(-1)
    rate_flat = well_rate.reshape(-1)
    cell_rate = (outflow + rate_flat) / volume_flat
    rate_top = lax.pmax(jnp.max(cell_rate), ("wide", "narrow"))
    time_step = courant / rate_top
    conc_next = conc_flat + time_step / volume_flat * (
        rate_flat * (inject_conc.reshape(-1) - conc_flat) - advection
    )
    return (pressure_next, conc_next.reshape(owned_count, -1))


def solution(mesh):
    return jax.shard_map(
        local,
        mesh=mesh,
        in_specs=(
            P(("wide", "narrow"), None),
            P(("wide", "narrow"), None),
            P(("wide", "narrow"), None),
            P(("wide", "narrow"), None),
            P(("wide", "narrow"), None),
            P(("wide", "narrow"), None),
            P(None, ("wide", "narrow")),
            P(None, ("wide", "narrow")),
            P(("wide", "narrow"), None, None, None),
            P(("wide", "narrow"), None),
            P(("wide", "narrow"), None, None),
            P(("wide", "narrow"), None),
            P(("wide", "narrow"), None),
            P(("wide", "narrow")),
            P(("wide", "narrow"), None),
        ),
        out_specs=(P(("wide", "narrow"), None), P(("wide", "narrow"), None)),
        check_vma=False,
    )
```

profile of v0, /device:TPU:0, one launch (start us, length us, event | category | flops | bytes accessed | tf_op | source)
XLA Modules:
  0.0 232.3 jit_solution(17184199817668447989)
XLA Ops:
  7.2 0.9 constant_dynamic-update-slice_fusion.4
  8.1 0.7 compare_select_fusion.3
  8.9 0.7 iota_compare_fusion
  10.3 4.9 %collective-permute-start = (bf16[8,128]{1,0:T(8,128)(2,1)S(1)}, bf16[8,128]{1,0:T(8,128)(2,1)S(1)}, u32[]{:S(2)}, u32[]{:S(2)}) collective-permute-start(bf16[8,128]{1,0:T(8,128)(2,1)S(1)} %get-tuple-element.29), channel_id=1, source_target_pairs={{0,8},{4,12},{8,16},{12,20},{16,24},{20,28},{1,9},{5,13},{9,17},{1... | collective-permute-start | bytes 6152 | tf_op jit(solution)/shard_map/ppermute | solution.py:14
  15.2 3.4 %collective-permute-start.1 = (bf16[8,128]{1,0:T(8,128)(2,1)S(1)}, bf16[8,128]{1,0:T(8,128)(2,1)S(1)}, u32[]{:S(2)}, u32[]{:S(2)}) collective-permute-start(bf16[8,128]{1,0:T(8,128)(2,1)S(1)} %get-tuple-element.28), channel_id=1, source_target_pairs={{0,4},{4,8},{8,12},{12,16},{16,20},{20,24},{24,28},{1,5},{5,9},{9,... | collective-permute-start | bytes 6152 | tf_op jit(solution)/shard_map/ppermute | solution.py:14
  18.6 1.3 collective-permute-start.2
  19.9 1.3 collective-permute-start.3
  21.2 0.7 compare_select_fusion.2
  21.9 0.7 compare_select_fusion.1
  22.6 0.7 compare_select_fusion.4
  23.5 3.2 %slice.70 = bf16[64,1,128,128]{3,2,1,0:T(8,128)(2,1)} slice(bf16[64,4,128,128]{3,2,1,0:T(8,128)(2,1)} %param.23), slice={[0:64], [0:1], [0:128], [0:128]} | slice | bytes 4194304 | tf_op jit(solution)/shard_map/slice | solution.py:80
  26.7 5.3 %copy.38 = bf16[64,1,128,128]{0,3,2,1:T(8,128)(2,1)} copy(bf16[64,1,128,128]{3,2,1,0:T(8,128)(2,1)} %slice.70) | data formatting | bytes 4194304
  32.1 1.9 gather_fusion.4
  34.4 0.9 gather_fusion.3
  35.2 5.7 %fusion.8 = f32[64,1,128,1]{2,1,3,0:T(1,128)S(1)} fusion(bf16[64,4,128,128]{3,2,1,0:T(8,128)(2,1)} %param.23, bf16[64,4,128,1]{2,1,0,3:T(4,128)(2,1)S(1)} %bitcast.134), kind=kOutput, calls=%fused_computation.23 | convolution fusion | flops 8388608 | bytes 8486912 | tf_op jit(solution)/shard_map/rkij,rkj->ri/dot_general | solution.py:19
  41.7 0.7 gather_fusion.1
  42.4 3.4 %fusion = f32[32,1,128,1]{2,1,3,0:T(1,128)S(1)} fusion(bf16[64,4,128,128]{3,2,1,0:T(8,128)(2,1)} %param.23, bf16[32,4,128,1]{2,1,0,3:T(4,128)(2,1)S(1)} %bitcast.143), kind=kOutput, calls=%fused_computation.14 | convolution fusion | flops 4194304 | bytes 4243456 | tf_op jit(solution)/shard_map/rkij,rkj->ri/dot_general | solution.py:19
  46.5 6.3 %collective-permute-start.4 = (bf16[8,128]{1,0:T(8,128)(2,1)S(1)}, bf16[8,128]{1,0:T(8,128)(2,1)S(1)}, u32[]{:S(2)}, u32[]{:S(2)}) collective-permute-start(bf16[8,128]{1,0:T(8,128)(2,1)S(1)} %get-tuple-element.25), channel_id=1, source_target_pairs={{0,8},{4,12},{8,16},{12,20},{16,24},{20,28},{1,9},{5,13},{9,17},{1... | collective-permute-start | bytes 6152 | tf_op jit(solution)/shard_map/ppermute | solution.py:14
  52.8 0.6 fusion.23
  53.5 2.0 scatter_custom_fusion
  55.4 40.0 %psum.7 = f32[4096]{0:T(1024)S(1)} all-reduce(f32[4096]{0:T(1024)S(1)} %scatter_custom_fusion), channel_id=1, replica_groups=mesh['wide'=8,'narrow'=4] {'wide','narrow'}, use_global_device_ids=true, to_apply=%region_1.2 | all-reduce | flops 4096 | bytes 32768 | tf_op jit(solution)/shard_map/psum | solution.py:90
  95.4 4.2 %collective-permute-start.5 = (bf16[8,128]{1,0:T(8,128)(2,1)S(1)}, bf16[8,128]{1,0:T(8,128)(2,1)S(1)}, u32[]{:S(2)}, u32[]{:S(2)}) collective-permute-start(bf16[8,128]{1,0:T(8,128)(2,1)S(1)} %get-tuple-element.24), channel_id=1, source_target_pairs={{0,4},{4,8},{8,12},{12,16},{16,20},{20,24},{24,28},{1,5},{5,9},{9,... | collective-permute-start | bytes 6152 | tf_op jit(solution)/shard_map/ppermute | solution.py:14
  99.6 1.3 collective-permute-start.6
  100.9 1.5 collective-permute-start.7
  102.5 2.6 %collective-permute-done.6 = bf16[8,128]{1,0:T(8,128)(2,1)S(1)} collective-permute-done((bf16[8,128]{1,0:T(8,128)(2,1)S(1)}, bf16[8,128]{1,0:T(8,128)(2,1)S(1)}, u32[]{:S(2)}, u32[]{:S(2)}) %collective-permute-start.6) | collective-permute-done | bytes 2080 | tf_op jit(solution)/shard_map/ppermute | solution.py:14
  105.1 1.4 collective-permute-done.7
  106.5 0.9 gather_fusion.5
  107.4 5.6 %fusion.6 = f32[64,1,128,1]{2,1,3,0:T(1,128)S(1)} fusion(bf16[64,4,128,128]{3,2,1,0:T(8,128)(2,1)} %param.23, bf16[64,4,128,1]{2,1,0,3:T(4,128)(2,1)S(1)} %bitcast.135), kind=kOutput, calls=%fused_computation.21 | convolution fusion | flops 8388608 | bytes 8486912 | tf_op jit(solution)/shard_map/rkij,rkj->ri/dot_general | solution.py:19
  113.0 0.9 gather_fusion.6
  113.9 5.6 %fusion.4 = f32[64,1,128,1]{2,1,3,0:T(1,128)S(1)} fusion(bf16[64,4,128,128]{3,2,1,0:T(8,128)(2,1)} %param.23, bf16[64,4,128,1]{2,1,0,3:T(4,128)(2,1)S(1)} %bitcast.136), kind=kOutput, calls=%fused_computation.19 | convolution fusion | flops 8388608 | bytes 8486912 | tf_op jit(solution)/shard_map/rkij,rkj->ri/dot_general | solution.py:19
  119.6 0.9 gather_fusion.7
  120.5 5.6 %fusion.2 = f32[64,1,128,1]{2,1,3,0:T(1,128)S(1)} fusion(bf16[64,4,128,128]{3,2,1,0:T(8,128)(2,1)} %param.23, bf16[64,4,128,1]{2,1,0,3:T(4,128)(2,1)S(1)} %bitcast.133), kind=kOutput, calls=%fused_computation.17 | convolution fusion | flops 8388608 | bytes 8486912 | tf_op jit(solution)/shard_map/rkij,rkj->ri/dot_general | solution.py:19
  126.1 2.2 convolution_bitcast_fusion
  128.3 26.0 %all-gather = bf16[8,1,512]{2,1,0:T(2,128)(2,1)S(1)} all-gather(bf16[1,1,512]{2,1,0:T(2,128)(2,1)S(1)} %convolution_bitcast_fusion), channel_id=1, replica_groups=mesh['wide'=8,'narrow'=4] {'wide'}, dimensions={0}, use_global_device_ids=true | all-gather | bytes 9216 | tf_op jit(solution)/shard_map/all_gather | solution.py:96
  154.4 1.9 gather_fusion.8
  157.4 2.1 collective-permute-start.8
  159.5 1.8 collective-permute-start.9
  161.3 1.3 collective-permute-start.10
  162.6 1.3 collective-permute-start.11
  163.9 6.5 %collective-permute-start.12 = (f32[8,128]{1,0:T(8,128)S(1)}, f32[8,128]{1,0:T(8,128)S(1)}, u32[]{:S(2)}, u32[]{:S(2)}) collective-permute-start(f32[8,128]{1,0:T(8,128)S(1)} %get-tuple-element.17), channel_id=1, source_target_pairs={{0,8},{4,12},{8,16},{12,20},{16,24},{20,28},{1,9},{5,13},{9,17},{1... | collective-permute-start | bytes 12296 | tf_op jit(solution)/shard_map/ppermute | solution.py:14
  170.4 2.6 %collective-permute-start.13 = (f32[8,128]{1,0:T(8,128)S(1)}, f32[8,128]{1,0:T(8,128)S(1)}, u32[]{:S(2)}, u32[]{:S(2)}) collective-permute-start(f32[8,128]{1,0:T(8,128)S(1)} %get-tuple-element.16), channel_id=1, source_target_pairs={{0,4},{4,8},{8,12},{12,16},{16,20},{20,24},{24,28},{1,5},{5,9},{9,... | collective-permute-start | bytes 12296 | tf_op jit(solution)/shard_map/ppermute | solution.py:14
  173.1 1.3 collective-permute-start.14
  174.4 1.3 collective-permute-start.15
  175.8 3.5 %collective-permute-done.14 = f32[8,128]{1,0:T(8,128)S(1)} collective-permute-done((f32[8,128]{1,0:T(8,128)S(1)}, f32[8,128]{1,0:T(8,128)S(1)}, u32[]{:S(2)}, u32[]{:S(2)}) %collective-permute-start.14) | collective-permute-done | bytes 4128 | tf_op jit(solution)/shard_map/ppermute | solution.py:14
  179.3 0.7 gather_fusion.10
  180.0 2.7 %collective-permute-done.15 = f32[8,128]{1,0:T(8,128)S(1)} collective-permute-done((f32[8,128]{1,0:T(8,128)S(1)}, f32[8,128]{1,0:T(8,128)S(1)}, u32[]{:S(2)}, u32[]{:S(2)}) %collective-permute-start.15) | collective-permute-done | bytes 4128 | tf_op jit(solution)/shard_map/ppermute | solution.py:14
  182.7 0.7 gather_fusion.12
  184.2 39.9 %pmax.7 = f32[]{:T(128)} all-reduce(f32[]{:T(128)} %fusion.16), channel_id=1, replica_groups=mesh['wide'=8,'narrow'=4] {'wide','narrow'}, use_global_device_ids=true, to_apply=%region_4.5 | all-reduce | flops 1 | bytes 8 | tf_op jit(solution)/shard_map/pmax | solution.py:119
  (96 shorter events, 5.6 us)
Async XLA Ops:
  7.2 45.6 %copy-start = (bf16[256,4096]{1,0:T(8,128)(2,1)S(1)}, bf16[256,4096]{1,0:T(8,128)(2,1)}, u32[]{:S(2)}) copy-start(bf16[256,4096]{1,0:T(8,128)(2,1)} %param.27) | copy-start | bytes 6291460
  7.2 118.9 %all-gather.3.cloned.1.call-start = ((), (), s32[]{:S(2)}) async-start(), calls=%async_computation | async-start | bytes 1310720 | tf_op jit(solution)/shard_map/all_gather | solution.py:94
  10.3 31.3 %collective-permute-start = (bf16[8,128]{1,0:T(8,128)(2,1)S(1)}, bf16[8,128]{1,0:T(8,128)(2,1)S(1)}, u32[]{:S(2)}, u32[]{:S(2)}) collective-permute-start(bf16[8,128]{1,0:T(8,128)(2,1)S(1)} %get-tuple-element.29), channel_id=1, source_target_pairs={{0,8},{4,12},{8,16},{12,20},{16,24},{20,28},{1,9},{5,13},{9,17},{1... | collective-permute-start | bytes 6152 | tf_op jit(solution)/shard_map/ppermute | solution.py:14
  15.2 26.4 %collective-permute-start.1 = (bf16[8,128]{1,0:T(8,128)(2,1)S(1)}, bf16[8,128]{1,0:T(8,128)(2,1)S(1)}, u32[]{:S(2)}, u32[]{:S(2)}) collective-permute-start(bf16[8,128]{1,0:T(8,128)(2,1)S(1)} %get-tuple-element.28), channel_id=1, source_target_pairs={{0,4},{4,8},{8,12},{12,16},{16,20},{20,24},{24,28},{1,5},{5,9},{9,... | collective-permute-start | bytes 6152 | tf_op jit(solution)/shard_map/ppermute | solution.py:14
  18.6 23.0 %collective-permute-start.2 = (bf16[8,128]{1,0:T(8,128)(2,1)S(1)}, bf16[8,128]{1,0:T(8,128)(2,1)S(1)}, u32[]{:S(2)}, u32[]{:S(2)}) collective-permute-start(bf16[8,128]{1,0:T(8,128)(2,1)S(1)} %get-tuple-element.27), channel_id=1, source_target_pairs={{4,0},{8,4},{12,8},{16,12},{20,16},{24,20},{28,24},{5,1},{9,5},{13... | collective-permute-start | bytes 6152 | tf_op jit(solution)/shard_map/ppermute | solution.py:14
  19.9 21.8 %collective-permute-start.3 = (bf16[8,128]{1,0:T(8,128)(2,1)S(1)}, bf16[8,128]{1,0:T(8,128)(2,1)S(1)}, u32[]{:S(2)}, u32[]{:S(2)}) collective-permute-start(bf16[8,128]{1,0:T(8,128)(2,1)S(1)} %get-tuple-element.26), channel_id=1, source_target_pairs={{8,0},{12,4},{16,8},{20,12},{24,16},{28,20},{9,1},{13,5},{17,9},{2... | collective-permute-start | bytes 6152 | tf_op jit(solution)/shard_map/ppermute | solution.py:14
  26.7 14.2 %copy-start.9 = (s32[6,32]{1,0:T(8,128)S(1)}, s32[6,32]{1,0:T(8,128)}, u32[]{:S(2)}) copy-start(s32[6,32]{1,0:T(8,128)} %param.22) | copy-start | bytes 2308
  26.7 14.3 %copy-start.1 = (f32[32,128]{1,0:T(8,128)S(1)}, f32[32,128]{1,0:T(8,128)}, u32[]{:S(2)}) copy-start(f32[32,128]{1,0:T(8,128)} %param.17) | copy-start | bytes 49156
  32.1 13.7 %copy-start.7 = (f32[32,128]{1,0:T(8,128)S(1)}, f32[32,128]{1,0:T(8,128)}, u32[]{:S(2)}) copy-start(f32[32,128]{1,0:T(8,128)} %param.16) | copy-start | bytes 49156
  46.5 56.0 %collective-permute-start.4 = (bf16[8,128]{1,0:T(8,128)(2,1)S(1)}, bf16[8,128]{1,0:T(8,128)(2,1)S(1)}, u32[]{:S(2)}, u32[]{:S(2)}) collective-permute-start(bf16[8,128]{1,0:T(8,128)(2,1)S(1)} %get-tuple-element.25), channel_id=1, source_target_pairs={{0,8},{4,12},{8,16},{12,20},{16,24},{20,28},{1,9},{5,13},{9,17},{1... | collective-permute-start | bytes 6152 | tf_op jit(solution)/shard_map/ppermute | solution.py:14
  95.4 7.1 %collective-permute-start.5 = (bf16[8,128]{1,0:T(8,128)(2,1)S(1)}, bf16[8,128]{1,0:T(8,128)(2,1)S(1)}, u32[]{:S(2)}, u32[]{:S(2)}) collective-permute-start(bf16[8,128]{1,0:T(8,128)(2,1)S(1)} %get-tuple-element.24), channel_id=1, source_target_pairs={{0,4},{4,8},{8,12},{12,16},{16,20},{20,24},{24,28},{1,5},{5,9},{9,... | collective-permute-start | bytes 6152 | tf_op jit(solution)/shard_map/ppermute | solution.py:14
  99.6 5.5 %collective-permute-start.6 = (bf16[8,128]{1,0:T(8,128)(2,1)S(1)}, bf16[8,128]{1,0:T(8,128)(2,1)S(1)}, u32[]{:S(2)}, u32[]{:S(2)}) collective-permute-start(bf16[8,128]{1,0:T(8,128)(2,1)S(1)} %get-tuple-element.23), channel_id=1, source_target_pairs={{4,0},{8,4},{12,8},{16,12},{20,16},{24,20},{28,24},{5,1},{9,5},{13... | collective-permute-start | bytes 6152 | tf_op jit(solution)/shard_map/ppermute | solution.py:14
  100.9 5.6 %collective-permute-start.7 = (bf16[8,128]{1,0:T(8,128)(2,1)S(1)}, bf16[8,128]{1,0:T(8,128)(2,1)S(1)}, u32[]{:S(2)}, u32[]{:S(2)}) collective-permute-start(bf16[8,128]{1,0:T(8,128)(2,1)S(1)} %get-tuple-element.22), channel_id=1, source_target_pairs={{8,0},{12,4},{16,8},{20,12},{24,16},{28,20},{9,1},{13,5},{17,9},{2... | collective-permute-start | bytes 6152 | tf_op jit(solution)/shard_map/ppermute | solution.py:14
  119.5 37.2 %copy-start.6 = (f32[32,128]{1,0:T(8,128)S(1)}, f32[32,128]{1,0:T(8,128)}, u32[]{:S(2)}) copy-start(f32[32,128]{1,0:T(8,128)} %param.15) | copy-start | bytes 49156
  119.5 63.9 %copy-start.3 = (f32[6,4096]{1,0:T(8,128)S(1)}, f32[6,4096]{1,0:T(8,128)}, u32[]{:S(2)}) copy-start(f32[6,4096]{1,0:T(8,128)} %param.21) | copy-start | bytes 294916
  119.5 64.0 %copy-start.4 = (f32[32,128]{1,0:T(8,128)S(1)}, f32[32,128]{1,0:T(8,128)}, u32[]{:S(2)}) copy-start(f32[32,128]{1,0:T(8,128)} %param.19) | copy-start | bytes 49156
  119.5 64.0 %copy-start.5 = (f32[32,128]{1,0:T(8,128)S(1)}, f32[32,128]{1,0:T(8,128)}, u32[]{:S(2)}) copy-start(f32[32,128]{1,0:T(8,128)} %param.18) | copy-start | bytes 49156
  119.6 105.2 %copy-start.8 = (f32[32,128]{1,0:T(8,128)S(1)}, f32[32,128]{1,0:T(8,128)}, u32[]{:S(2)}) copy-start(f32[32,128]{1,0:T(8,128)} %param.20) | copy-start | bytes 49156
  156.7 68.7 %copy-start.2 = (f32[32,128]{1,0:T(8,128)}, f32[32,128]{1,0:T(8,128)S(1)}, u32[]{:S(2)}) copy-start(f32[32,128]{1,0:T(8,128)S(1)} %get-tuple-element.5) | copy-start | bytes 49156
  157.4 13.0 %collective-permute-start.8 = (f32[8,128]{1,0:T(8,128)S(1)}, f32[8,128]{1,0:T(8,128)S(1)}, u32[]{:S(2)}, u32[]{:S(2)}) collective-permute-start(f32[8,128]{1,0:T(8,128)S(1)} %get-tuple-element.21), channel_id=1, source_target_pairs={{0,8},{4,12},{8,16},{12,20},{16,24},{20,28},{1,9},{5,13},{9,17},{1... | collective-permute-start | bytes 12296 | tf_op jit(solution)/shard_map/ppermute | solution.py:14
  159.5 13.5 %collective-permute-start.9 = (f32[8,128]{1,0:T(8,128)S(1)}, f32[8,128]{1,0:T(8,128)S(1)}, u32[]{:S(2)}, u32[]{:S(2)}) collective-permute-start(f32[8,128]{1,0:T(8,128)S(1)} %get-tuple-element.20), channel_id=1, source_target_pairs={{0,4},{4,8},{8,12},{12,16},{16,20},{20,24},{24,28},{1,5},{5,9},{9,... | collective-permute-start | bytes 12296 | tf_op jit(solution)/shard_map/ppermute | solution.py:14
  161.3 13.1 %collective-permute-start.10 = (f32[8,128]{1,0:T(8,128)S(1)}, f32[8,128]{1,0:T(8,128)S(1)}, u32[]{:S(2)}, u32[]{:S(2)}) collective-permute-start(f32[8,128]{1,0:T(8,128)S(1)} %get-tuple-element.19), channel_id=1, source_target_pairs={{4,0},{8,4},{12,8},{16,12},{20,16},{24,20},{28,24},{5,1},{9,5},{13... | collective-permute-start | bytes 12296 | tf_op jit(solution)/shard_map/ppermute | solution.py:14
  162.6 13.1 %collective-permute-start.11 = (f32[8,128]{1,0:T(8,128)S(1)}, f32[8,128]{1,0:T(8,128)S(1)}, u32[]{:S(2)}, u32[]{:S(2)}) collective-permute-start(f32[8,128]{1,0:T(8,128)S(1)} %get-tuple-element.18), channel_id=1, source_target_pairs={{8,0},{12,4},{16,8},{20,12},{24,16},{28,20},{9,1},{13,5},{17,9},{2... | collective-permute-start | bytes 12296 | tf_op jit(solution)/shard_map/ppermute | solution.py:14
  163.9 11.8 %collective-permute-start.12 = (f32[8,128]{1,0:T(8,128)S(1)}, f32[8,128]{1,0:T(8,128)S(1)}, u32[]{:S(2)}, u32[]{:S(2)}) collective-permute-start(f32[8,128]{1,0:T(8,128)S(1)} %get-tuple-element.17), channel_id=1, source_target_pairs={{0,8},{4,12},{8,16},{12,20},{16,24},{20,28},{1,9},{5,13},{9,17},{1... | collective-permute-start | bytes 12296 | tf_op jit(solution)/shard_map/ppermute | solution.py:14
  170.4 5.3 %collective-permute-start.13 = (f32[8,128]{1,0:T(8,128)S(1)}, f32[8,128]{1,0:T(8,128)S(1)}, u32[]{:S(2)}, u32[]{:S(2)}) collective-permute-start(f32[8,128]{1,0:T(8,128)S(1)} %get-tuple-element.16), channel_id=1, source_target_pairs={{0,4},{4,8},{8,12},{12,16},{16,20},{20,24},{24,28},{1,5},{5,9},{9,... | collective-permute-start | bytes 12296 | tf_op jit(solution)/shard_map/ppermute | solution.py:14
  173.1 6.2 %collective-permute-start.14 = (f32[8,128]{1,0:T(8,128)S(1)}, f32[8,128]{1,0:T(8,128)S(1)}, u32[]{:S(2)}, u32[]{:S(2)}) collective-permute-start(f32[8,128]{1,0:T(8,128)S(1)} %get-tuple-element.15), channel_id=1, source_target_pairs={{4,0},{8,4},{12,8},{16,12},{20,16},{24,20},{28,24},{5,1},{9,5},{13... | collective-permute-start | bytes 12296 | tf_op jit(solution)/shard_map/ppermute | solution.py:14
  174.4 8.3 %collective-permute-start.15 = (f32[8,128]{1,0:T(8,128)S(1)}, f32[8,128]{1,0:T(8,128)S(1)}, u32[]{:S(2)}, u32[]{:S(2)}) collective-permute-start(f32[8,128]{1,0:T(8,128)S(1)} %get-tuple-element.14), channel_id=1, source_target_pairs={{8,0},{12,4},{16,8},{20,12},{24,16},{28,20},{9,1},{13,5},{17,9},{2... | collective-permute-start | bytes 12296 | tf_op jit(solution)/shard_map/ppermute | solution.py:14
Sparse Core Ops, SparseCore 0:
  21.3 20.1 all-gather.2
where the time goes:
time: 233 us; the launch traced here: 232 us
  blocking collectives  106 us (45%)
  starting transfers between devices  42.4 us (18%)
  matrix products  29.2 us (13%)
  local copies, waits for them, and re-layouts  21.3 us (9%)
  between operations  15.3 us (7%)
  waiting for transfers between devices  10.2 us (4%)
  other arithmetic  8.01 us (3%)
    ppermute x16, starting transfers between devices, from_behind(): lax.ppermute(value, axis, [(source, source + steps) for source in range(l...  42.3 us
    psum x1, blocking collectives, local(): summed = lax.psum(partial_value, ('wide', 'narrow'))  40 us
    pmax x1, blocking collectives, local(): rate_top = lax.pmax(jnp.max(cell_rate), ('wide', 'narrow'))  39.9 us
    all_gather x1, blocking collectives, local(): coarse_values = lax.all_gather(owner_values, 'wide', axis=0, tiled=True)  26 us
    dot_general x5, matrix products, block_product(): jnp.einsum('rkij,rkj->ri', matrix, picked, preferred_element_type=jnp.flo...  26 us
    ppermute x16, waiting for transfers between devices, from_behind(): lax.ppermute(value, axis, [(source, source + steps) for source in range(l...  10.2 us
    unnamed x35, local copies, waits for them, and re-layouts  5.47 us
  transfers between devices with their start and end apart: 17, of which 4 were waited for; matrix products, arithmetic and copies ran while one was open for 21% of the time, Pallas kernels for 0%

commit v1 on v0

--- a/solution.py
+++ b/solution.py
@@ -87,7 +87,7 @@
             / diagonal
         )
     partial_value = jnp.zeros((coarse_total,), jnp.float32).at[coarse_index].add(local_coarse)
-    summed = lax.psum(partial_value, ("wide", "narrow"))
+    summed = lax.psum(lax.psum(partial_value, "narrow"), "wide")
     owner_block = lax.dynamic_slice_in_dim(
         summed, lax.axis_index("wide") * coarse_width, coarse_width
     )

time: 233 us -> 236 us (1.013)
  blocking collectives: 106 us -> 111 us
  starting transfers between devices: 42.4 us -> 38.9 us
    psum x1 -> x2, blocking collectives: 40 us -> 45.1 us  [local(): summed = lax.psum(lax.psum(partial_value, 'narrow'), 'wide')]
    ppermute x16, starting transfers between devices: 42.3 us -> 38.9 us  [from_behind(): lax.ppermute(value, axis, [(source, source + steps) for source in range(l...]
  transfers between devices with their start and end apart: 17 -> 17, of which waited for: 4 -> 4; matrix products, arithmetic and copies ran while one was open for 21% -> 20% of each run, Pallas kernels for 0% -> 0%
where the time goes in v1:
time: 236 us; the launch traced here: 235 us
  blocking collectives  111 us (47%)
  starting transfers between devices  38.9 us (16%)
  matrix products  29.2 us (12%)
  local copies, waits for them, and re-layouts  21.3 us (9%)
  between operations  15.3 us (6%)
  waiting for transfers between devices  11.2 us (5%)
  other arithmetic  8.01 us (3%)
    psum x2, blocking collectives, local(): summed = lax.psum(lax.psum(partial_value, 'narrow'), 'wide')  45.1 us
    pmax x1, blocking collectives, local(): rate_top = lax.pmax(jnp.max(cell_rate), ('wide', 'narrow'))  39.9 us
    ppermute x16, starting transfers between devices, from_behind(): lax.ppermute(value, axis, [(source, source + steps) for source in range(l...  38.9 us
    all_gather x1, blocking collectives, local(): coarse_values = lax.all_gather(owner_values, 'wide', axis=0, tiled=True)  26 us
    dot_general x5, matrix products, block_product(): jnp.einsum('rkij,rkj->ri', matrix, picked, preferred_element_type=jnp.flo...  26 us
    ppermute x16, waiting for transfers between devices, from_behind(): lax.ppermute(value, axis, [(source, source + steps) for source in range(l...  11.2 us
    unnamed x35, local copies, waits for them, and re-layouts  5.49 us
  transfers between devices with their start and end apart: 17, of which 4 were waited for; matrix products, arithmetic and copies ran while one was open for 20% of the time, Pallas kernels for 0%

profile of v1, /device:TPU:0, one launch (start us, length us, event | category | flops | bytes accessed | tf_op | source)
XLA Modules:
  0.0 234.9 jit_solution(7274201922021182589)
XLA Ops:
  7.2 0.9 constant_dynamic-update-slice_fusion.4
  8.1 0.7 compare_select_fusion.3
  8.9 0.7 iota_compare_fusion
  10.3 4.9 %collective-permute-start = (bf16[8,128]{1,0:T(8,128)(2,1)S(1)}, bf16[8,128]{1,0:T(8,128)(2,1)S(1)}, u32[]{:S(2)}, u32[]{:S(2)}) collective-permute-start(bf16[8,128]{1,0:T(8,128)(2,1)S(1)} %get-tuple-element.29), channel_id=1, source_target_pairs={{0,8},{4,12},{8,16},{12,20},{16,24},{20,28},{1,9},{5,13},{9,17},{1... | collective-permute-start | bytes 6152 | tf_op jit(solution)/shard_map/ppermute | solution.py:14
  15.2 3.4 %collective-permute-start.1 = (bf16[8,128]{1,0:T(8,128)(2,1)S(1)}, bf16[8,128]{1,0:T(8,128)(2,1)S(1)}, u32[]{:S(2)}, u32[]{:S(2)}) collective-permute-start(bf16[8,128]{1,0:T(8,128)(2,1)S(1)} %get-tuple-element.28), channel_id=1, source_target_pairs={{0,4},{4,8},{8,12},{12,16},{16,20},{20,24},{24,28},{1,5},{5,9},{9,... | collective-permute-start | bytes 6152 | tf_op jit(solution)/shard_map/ppermute | solution.py:14
  18.6 1.3 collective-permute-start.2
  19.9 1.3 collective-permute-start.3
  21.2 0.7 compare_select_fusion.2
  21.9 0.7 compare_select_fusion.1
  22.6 0.7 compare_select_fusion.4
  23.5 3.2 %slice.70 = bf16[64,1,128,128]{3,2,1,0:T(8,128)(2,1)} slice(bf16[64,4,128,128]{3,2,1,0:T(8,128)(2,1)} %param.23), slice={[0:64], [0:1], [0:128], [0:128]} | slice | bytes 4194304 | tf_op jit(solution)/shard_map/slice | solution.py:80
  26.7 5.4 %copy.38 = bf16[64,1,128,128]{0,3,2,1:T(8,128)(2,1)} copy(bf16[64,1,128,128]{3,2,1,0:T(8,128)(2,1)} %slice.70) | data formatting | bytes 4194304
  32.1 2.0 gather_fusion.4
  34.4 0.9 gather_fusion.3
  35.2 5.7 %fusion.8 = f32[64,1,128,1]{2,1,3,0:T(1,128)S(1)} fusion(bf16[64,4,128,128]{3,2,1,0:T(8,128)(2,1)} %param.23, bf16[64,4,128,1]{2,1,0,3:T(4,128)(2,1)S(1)} %bitcast.134), kind=kOutput, calls=%fused_computation.23 | convolution fusion | flops 8388608 | bytes 8486912 | tf_op jit(solution)/shard_map/rkij,rkj->ri/dot_general | solution.py:19
  41.7 0.7 gather_fusion.1
  42.4 3.4 %fusion = f32[32,1,128,1]{2,1,3,0:T(1,128)S(1)} fusion(bf16[64,4,128,128]{3,2,1,0:T(8,128)(2,1)} %param.23, bf16[32,4,128,1]{2,1,0,3:T(4,128)(2,1)S(1)} %bitcast.143), kind=kOutput, calls=%fused_computation.14 | convolution fusion | flops 4194304 | bytes 4243456 | tf_op jit(solution)/shard_map/rkij,rkj->ri/dot_general | solution.py:19
  47.1 2.0 scatter_custom_fusion
  49.1 10.5 %psum.14 = f32[4096]{0:T(1024)S(1)} all-reduce(f32[4096]{0:T(1024)S(1)} %scatter_custom_fusion), channel_id=1, replica_groups=mesh['wide'=8,'narrow'=4] {'narrow'}, use_global_device_ids=true, to_apply=%region_1.2 | all-reduce | flops 4096 | bytes 32768 | tf_op jit(solution)/shard_map/psum | solution.py:90
  59.6 5.9 %collective-permute-start.4 = (bf16[8,128]{1,0:T(8,128)(2,1)S(1)}, bf16[8,128]{1,0:T(8,128)(2,1)S(1)}, u32[]{:S(2)}, u32[]{:S(2)}) collective-permute-start(bf16[8,128]{1,0:T(8,128)(2,1)S(1)} %get-tuple-element.25), channel_id=1, source_target_pairs={{0,8},{4,12},{8,16},{12,20},{16,24},{20,28},{1,9},{5,13},{9,17},{1... | collective-permute-start | bytes 6152 | tf_op jit(solution)/shard_map/ppermute | solution.py:14
  65.6 34.6 %psum.15 = f32[4096]{0:T(1024)S(1)} all-reduce(f32[4096]{0:T(1024)S(1)} %psum.14), channel_id=1, replica_groups=mesh['wide'=8,'narrow'=4] {'wide'}, use_global_device_ids=true, to_apply=%region_2.3 | all-reduce | flops 4096 | bytes 32768 | tf_op jit(solution)/shard_map/psum | solution.py:90
  100.2 1.3 collective-permute-start.5
  101.5 1.3 collective-permute-start.6
  102.8 1.5 collective-permute-start.7
  104.4 2.6 %collective-permute-done.6 = bf16[8,128]{1,0:T(8,128)(2,1)S(1)} collective-permute-done((bf16[8,128]{1,0:T(8,128)(2,1)S(1)}, bf16[8,128]{1,0:T(8,128)(2,1)S(1)}, u32[]{:S(2)}, u32[]{:S(2)}) %collective-permute-start.6) | collective-permute-done | bytes 2080 | tf_op jit(solution)/shard_map/ppermute | solution.py:14
  107.0 2.2 collective-permute-done.7
  109.2 0.9 gather_fusion.5
  110.0 5.6 %fusion.6 = f32[64,1,128,1]{2,1,3,0:T(1,128)S(1)} fusion(bf16[64,4,128,128]{3,2,1,0:T(8,128)(2,1)} %param.23, bf16[64,4,128,1]{2,1,0,3:T(4,128)(2,1)S(1)} %bitcast.135), kind=kOutput, calls=%fused_computation.21 | convolution fusion | flops 8388608 | bytes 8486912 | tf_op jit(solution)/shard_map/rkij,rkj->ri/dot_general | solution.py:19
  115.7 0.9 gather_fusion.6
  116.6 5.6 %fusion.4 = f32[64,1,128,1]{2,1,3,0:T(1,128)S(1)} fusion(bf16[64,4,128,128]{3,2,1,0:T(8,128)(2,1)} %param.23, bf16[64,4,128,1]{2,1,0,3:T(4,128)(2,1)S(1)} %bitcast.136), kind=kOutput, calls=%fused_computation.19 | convolution fusion | flops 8388608 | bytes 8486912 | tf_op jit(solution)/shard_map/rkij,rkj->ri/dot_general | solution.py:19
  122.3 0.9 gather_fusion.7
  123.2 5.6 %fusion.2 = f32[64,1,128,1]{2,1,3,0:T(1,128)S(1)} fusion(bf16[64,4,128,128]{3,2,1,0:T(8,128)(2,1)} %param.23, bf16[64,4,128,1]{2,1,0,3:T(4,128)(2,1)S(1)} %bitcast.133), kind=kOutput, calls=%fused_computation.17 | convolution fusion | flops 8388608 | bytes 8486912 | tf_op jit(solution)/shard_map/rkij,rkj->ri/dot_general | solution.py:19
  128.8 2.2 convolution_bitcast_fusion
  131.0 26.0 %all-gather = bf16[8,1,512]{2,1,0:T(2,128)(2,1)S(1)} all-gather(bf16[1,1,512]{2,1,0:T(2,128)(2,1)S(1)} %convolution_bitcast_fusion), channel_id=1, replica_groups=mesh['wide'=8,'narrow'=4] {'wide'}, dimensions={0}, use_global_device_ids=true | all-gather | bytes 9216 | tf_op jit(solution)/shard_map/all_gather | solution.py:96
  157.1 1.9 gather_fusion.8
  160.1 2.1 collective-permute-start.8
  162.2 1.3 collective-permute-start.9
  163.5 1.3 collective-permute-start.10
  164.8 1.3 collective-permute-start.11
  166.1 6.9 %collective-permute-start.12 = (f32[8,128]{1,0:T(8,128)S(1)}, f32[8,128]{1,0:T(8,128)S(1)}, u32[]{:S(2)}, u32[]{:S(2)}) collective-permute-start(f32[8,128]{1,0:T(8,128)S(1)} %get-tuple-element.17), channel_id=1, source_target_pairs={{0,8},{4,12},{8,16},{12,20},{16,24},{20,28},{1,9},{5,13},{9,17},{1... | collective-permute-start | bytes 12296 | tf_op jit(solution)/shard_map/ppermute | solution.py:14
  173.1 2.5 %collective-permute-start.13 = (f32[8,128]{1,0:T(8,128)S(1)}, f32[8,128]{1,0:T(8,128)S(1)}, u32[]{:S(2)}, u32[]{:S(2)}) collective-permute-start(f32[8,128]{1,0:T(8,128)S(1)} %get-tuple-element.16), channel_id=1, source_target_pairs={{0,4},{4,8},{8,12},{12,16},{16,20},{20,24},{24,28},{1,5},{5,9},{9,... | collective-permute-start | bytes 12296 | tf_op jit(solution)/shard_map/ppermute | solution.py:14
  175.6 1.3 collective-permute-start.14
  176.9 1.3 collective-permute-start.15
  178.3 3.7 %collective-permute-done.14 = f32[8,128]{1,0:T(8,128)S(1)} collective-permute-done((f32[8,128]{1,0:T(8,128)S(1)}, f32[8,128]{1,0:T(8,128)S(1)}, u32[]{:S(2)}, u32[]{:S(2)}) %collective-permute-start.14) | collective-permute-done | bytes 4128 | tf_op jit(solution)/shard_map/ppermute | solution.py:14
  182.0 0.7 gather_fusion.10
  182.7 2.7 %collective-permute-done.15 = f32[8,128]{1,0:T(8,128)S(1)} collective-permute-done((f32[8,128]{1,0:T(8,128)S(1)}, f32[8,128]{1,0:T(8,128)S(1)}, u32[]{:S(2)}, u32[]{:S(2)}) %collective-permute-start.15) | collective-permute-done | bytes 4128 | tf_op jit(solution)/shard_map/ppermute | solution.py:14
  185.4 0.7 gather_fusion.12
  186.9 39.9 %pmax.7 = f32[]{:T(128)} all-reduce(f32[]{:T(128)} %fusion.16), channel_id=1, replica_groups=mesh['wide'=8,'narrow'=4] {'wide','narrow'}, use_global_device_ids=true, to_apply=%region_5.6 | all-reduce | flops 1 | bytes 8 | tf_op jit(solution)/shard_map/pmax | solution.py:119
  (97 shorter events, 6.2 us)
Async XLA Ops:
  7.2 39.3 %copy-start = (bf16[256,4096]{1,0:T(8,128)(2,1)S(1)}, bf16[256,4096]{1,0:T(8,128)(2,1)}, u32[]{:S(2)}) copy-start(bf16[256,4096]{1,0:T(8,128)(2,1)} %param.27) | copy-start | bytes 6291460
  7.2 121.6 %all-gather.3.cloned.1.call-start = ((), (), s32[]{:S(2)}) async-start(), calls=%async_computation | async-start | bytes 1310720 | tf_op jit(solution)/shard_map/all_gather | solution.py:94
  10.3 31.4 %collective-permute-start = (bf16[8,128]{1,0:T(8,128)(2,1)S(1)}, bf16[8,128]{1,0:T(8,128)(2,1)S(1)}, u32[]{:S(2)}, u32[]{:S(2)}) collective-permute-start(bf16[8,128]{1,0:T(8,128)(2,1)S(1)} %get-tuple-element.29), channel_id=1, source_target_pairs={{0,8},{4,12},{8,16},{12,20},{16,24},{20,28},{1,9},{5,13},{9,17},{1... | collective-permute-start | bytes 6152 | tf_op jit(solution)/shard_map/ppermute | solution.py:14
  15.2 26.4 %collective-permute-start.1 = (bf16[8,128]{1,0:T(8,128)(2,1)S(1)}, bf16[8,128]{1,0:T(8,128)(2,1)S(1)}, u32[]{:S(2)}, u32[]{:S(2)}) collective-permute-start(bf16[8,128]{1,0:T(8,128)(2,1)S(1)} %get-tuple-element.28), channel_id=1, source_target_pairs={{0,4},{4,8},{8,12},{12,16},{16,20},{20,24},{24,28},{1,5},{5,9},{9,... | collective-permute-start | bytes 6152 | tf_op jit(solution)/shard_map/ppermute | solution.py:14
  18.6 23.1 %collective-permute-start.2 = (bf16[8,128]{1,0:T(8,128)(2,1)S(1)}, bf16[8,128]{1,0:T(8,128)(2,1)S(1)}, u32[]{:S(2)}, u32[]{:S(2)}) collective-permute-start(bf16[8,128]{1,0:T(8,128)(2,1)S(1)} %get-tuple-element.27), channel_id=1, source_target_pairs={{4,0},{8,4},{12,8},{16,12},{20,16},{24,20},{28,24},{5,1},{9,5},{13... | collective-permute-start | bytes 6152 | tf_op jit(solution)/shard_map/ppermute | solution.py:14
  19.9 21.8 %collective-permute-start.3 = (bf16[8,128]{1,0:T(8,128)(2,1)S(1)}, bf16[8,128]{1,0:T(8,128)(2,1)S(1)}, u32[]{:S(2)}, u32[]{:S(2)}) collective-permute-start(bf16[8,128]{1,0:T(8,128)(2,1)S(1)} %get-tuple-element.26), channel_id=1, source_target_pairs={{8,0},{12,4},{16,8},{20,12},{24,16},{28,20},{9,1},{13,5},{17,9},{2... | collective-permute-start | bytes 6152 | tf_op jit(solution)/shard_map/ppermute | solution.py:14
  26.7 14.2 %copy-start.9 = (s32[6,32]{1,0:T(8,128)S(1)}, s32[6,32]{1,0:T(8,128)}, u32[]{:S(2)}) copy-start(s32[6,32]{1,0:T(8,128)} %param.22) | copy-start | bytes 2308
  26.7 14.3 %copy-start.1 = (f32[32,128]{1,0:T(8,128)S(1)}, f32[32,128]{1,0:T(8,128)}, u32[]{:S(2)}) copy-start(f32[32,128]{1,0:T(8,128)} %param.17) | copy-start | bytes 49156
  32.1 13.7 %copy-start.7 = (f32[32,128]{1,0:T(8,128)S(1)}, f32[32,128]{1,0:T(8,128)}, u32[]{:S(2)}) copy-start(f32[32,128]{1,0:T(8,128)} %param.16) | copy-start | bytes 49156
  59.6 44.7 %collective-permute-start.4 = (bf16[8,128]{1,0:T(8,128)(2,1)S(1)}, bf16[8,128]{1,0:T(8,128)(2,1)S(1)}, u32[]{:S(2)}, u32[]{:S(2)}) collective-permute-start(bf16[8,128]{1,0:T(8,128)(2,1)S(1)} %get-tuple-element.25), channel_id=1, source_target_pairs={{0,8},{4,12},{8,16},{12,20},{16,24},{20,28},{1,9},{5,13},{9,17},{1... | collective-permute-start | bytes 6152 | tf_op jit(solution)/shard_map/ppermute | solution.py:14
  100.2 4.2 %collective-permute-start.5 = (bf16[8,128]{1,0:T(8,128)(2,1)S(1)}, bf16[8,128]{1,0:T(8,128)(2,1)S(1)}, u32[]{:S(2)}, u32[]{:S(2)}) collective-permute-start(bf16[8,128]{1,0:T(8,128)(2,1)S(1)} %get-tuple-element.24), channel_id=1, source_target_pairs={{0,4},{4,8},{8,12},{12,16},{16,20},{20,24},{24,28},{1,5},{5,9},{9,... | collective-permute-start | bytes 6152 | tf_op jit(solution)/shard_map/ppermute | solution.py:14
  101.5 5.5 %collective-permute-start.6 = (bf16[8,128]{1,0:T(8,128)(2,1)S(1)}, bf16[8,128]{1,0:T(8,128)(2,1)S(1)}, u32[]{:S(2)}, u32[]{:S(2)}) collective-permute-start(bf16[8,128]{1,0:T(8,128)(2,1)S(1)} %get-tuple-element.23), channel_id=1, source_target_pairs={{4,0},{8,4},{12,8},{16,12},{20,16},{24,20},{28,24},{5,1},{9,5},{13... | collective-permute-start | bytes 6152 | tf_op jit(solution)/shard_map/ppermute | solution.py:14
  102.8 6.4 %collective-permute-start.7 = (bf16[8,128]{1,0:T(8,128)(2,1)S(1)}, bf16[8,128]{1,0:T(8,128)(2,1)S(1)}, u32[]{:S(2)}, u32[]{:S(2)}) collective-permute-start(bf16[8,128]{1,0:T(8,128)(2,1)S(1)} %get-tuple-element.22), channel_id=1, source_target_pairs={{8,0},{12,4},{16,8},{20,12},{24,16},{28,20},{9,1},{13,5},{17,9},{2... | collective-permute-start | bytes 6152 | tf_op jit(solution)/shard_map/ppermute | solution.py:14
  122.2 37.2 %copy-start.6 = (f32[32,128]{1,0:T(8,128)S(1)}, f32[32,128]{1,0:T(8,128)}, u32[]{:S(2)}) copy-start(f32[32,128]{1,0:T(8,128)} %param.15) | copy-start | bytes 49156
  122.2 63.9 %copy-start.3 = (f32[6,4096]{1,0:T(8,128)S(1)}, f32[6,4096]{1,0:T(8,128)}, u32[]{:S(2)}) copy-start(f32[6,4096]{1,0:T(8,128)} %param.21) | copy-start | bytes 294916
  122.2 64.0 %copy-start.4 = (f32[32,128]{1,0:T(8,128)S(1)}, f32[32,128]{1,0:T(8,128)}, u32[]{:S(2)}) copy-start(f32[32,128]{1,0:T(8,128)} %param.19) | copy-start | bytes 49156
  122.2 64.0 %copy-start.5 = (f32[32,128]{1,0:T(8,128)S(1)}, f32[32,128]{1,0:T(8,128)}, u32[]{:S(2)}) copy-start(f32[32,128]{1,0:T(8,128)} %param.18) | copy-start | bytes 49156
  122.3 105.2 %copy-start.8 = (f32[32,128]{1,0:T(8,128)S(1)}, f32[32,128]{1,0:T(8,128)}, u32[]{:S(2)}) copy-start(f32[32,128]{1,0:T(8,128)} %param.20) | copy-start | bytes 49156
  159.4 68.7 %copy-start.2 = (f32[32,128]{1,0:T(8,128)}, f32[32,128]{1,0:T(8,128)S(1)}, u32[]{:S(2)}) copy-start(f32[32,128]{1,0:T(8,128)S(1)} %get-tuple-element.5) | copy-start | bytes 49156
  160.1 13.0 %collective-permute-start.8 = (f32[8,128]{1,0:T(8,128)S(1)}, f32[8,128]{1,0:T(8,128)S(1)}, u32[]{:S(2)}, u32[]{:S(2)}) collective-permute-start(f32[8,128]{1,0:T(8,128)S(1)} %get-tuple-element.21), channel_id=1, source_target_pairs={{0,8},{4,12},{8,16},{12,20},{16,24},{20,28},{1,9},{5,13},{9,17},{1... | collective-permute-start | bytes 12296 | tf_op jit(solution)/shard_map/ppermute | solution.py:14
  162.2 13.4 %collective-permute-start.9 = (f32[8,128]{1,0:T(8,128)S(1)}, f32[8,128]{1,0:T(8,128)S(1)}, u32[]{:S(2)}, u32[]{:S(2)}) collective-permute-start(f32[8,128]{1,0:T(8,128)S(1)} %get-tuple-element.20), channel_id=1, source_target_pairs={{0,4},{4,8},{8,12},{12,16},{16,20},{20,24},{24,28},{1,5},{5,9},{9,... | collective-permute-start | bytes 12296 | tf_op jit(solution)/shard_map/ppermute | solution.py:14
  163.5 13.4 %collective-permute-start.10 = (f32[8,128]{1,0:T(8,128)S(1)}, f32[8,128]{1,0:T(8,128)S(1)}, u32[]{:S(2)}, u32[]{:S(2)}) collective-permute-start(f32[8,128]{1,0:T(8,128)S(1)} %get-tuple-element.19), channel_id=1, source_target_pairs={{4,0},{8,4},{12,8},{16,12},{20,16},{24,20},{28,24},{5,1},{9,5},{13... | collective-permute-start | bytes 12296 | tf_op jit(solution)/shard_map/ppermute | solution.py:14
  164.8 13.4 %collective-permute-start.11 = (f32[8,128]{1,0:T(8,128)S(1)}, f32[8,128]{1,0:T(8,128)S(1)}, u32[]{:S(2)}, u32[]{:S(2)}) collective-permute-start(f32[8,128]{1,0:T(8,128)S(1)} %get-tuple-element.18), channel_id=1, source_target_pairs={{8,0},{12,4},{16,8},{20,12},{24,16},{28,20},{9,1},{13,5},{17,9},{2... | collective-permute-start | bytes 12296 | tf_op jit(solution)/shard_map/ppermute | solution.py:14
  166.1 12.1 %collective-permute-start.12 = (f32[8,128]{1,0:T(8,128)S(1)}, f32[8,128]{1,0:T(8,128)S(1)}, u32[]{:S(2)}, u32[]{:S(2)}) collective-permute-start(f32[8,128]{1,0:T(8,128)S(1)} %get-tuple-element.17), channel_id=1, source_target_pairs={{0,8},{4,12},{8,16},{12,20},{16,24},{20,28},{1,9},{5,13},{9,17},{1... | collective-permute-start | bytes 12296 | tf_op jit(solution)/shard_map/ppermute | solution.py:14
  173.1 5.2 %collective-permute-start.13 = (f32[8,128]{1,0:T(8,128)S(1)}, f32[8,128]{1,0:T(8,128)S(1)}, u32[]{:S(2)}, u32[]{:S(2)}) collective-permute-start(f32[8,128]{1,0:T(8,128)S(1)} %get-tuple-element.16), channel_id=1, source_target_pairs={{0,4},{4,8},{8,12},{12,16},{16,20},{20,24},{24,28},{1,5},{5,9},{9,... | collective-permute-start | bytes 12296 | tf_op jit(solution)/shard_map/ppermute | solution.py:14
  175.6 6.4 %collective-permute-start.14 = (f32[8,128]{1,0:T(8,128)S(1)}, f32[8,128]{1,0:T(8,128)S(1)}, u32[]{:S(2)}, u32[]{:S(2)}) collective-permute-start(f32[8,128]{1,0:T(8,128)S(1)} %get-tuple-element.15), channel_id=1, source_target_pairs={{4,0},{8,4},{12,8},{16,12},{20,16},{24,20},{28,24},{5,1},{9,5},{13... | collective-permute-start | bytes 12296 | tf_op jit(solution)/shard_map/ppermute | solution.py:14
  176.9 8.5 %collective-permute-start.15 = (f32[8,128]{1,0:T(8,128)S(1)}, f32[8,128]{1,0:T(8,128)S(1)}, u32[]{:S(2)}, u32[]{:S(2)}) collective-permute-start(f32[8,128]{1,0:T(8,128)S(1)} %get-tuple-element.14), channel_id=1, source_target_pairs={{8,0},{12,4},{16,8},{20,12},{24,16},{28,20},{9,1},{13,5},{17,9},{2... | collective-permute-start | bytes 12296 | tf_op jit(solution)/shard_map/ppermute | solution.py:14
Sparse Core Ops, SparseCore 0:
  21.3 20.1 all-gather.2
